TPU v7x, 32 devices: a whole 2x2x4 slice. The times are simulated.
32 devices in a mesh: ha: 8 (over z, core), wa: 4 (over y, x).
Axes of the slice: x: 2, y: 2, z: 4, core: 2. Of those that a mesh axis runs over, the one named last changes fastest.
Arguments:
- latents: bfloat16 [64, 64, 64, 512], P('ha', 'wa'), may hold values from -8 to 8
- cotangent: bfloat16 [64, 64, 64, 512], P('ha', 'wa'), may hold values from -0.59765625 to 0.59765625
- w_down: bfloat16 [512, 18], replicated, may hold values from -0.25 to 0.25
- bit_bias: float32 [18], replicated, may hold values from -1.5 to 1.5
- w_up: bfloat16 [18, 512], replicated, may hold values from -1.5 to 1.5
Outputs:
- grad_latents: bfloat16 [64, 64, 64, 512], P('ha', 'wa')
- bit_entropy: float32 [64, 64, 64], P('ha', 'wa')
- marginal: float32 [18], replicated
- grad_down: float32 [512, 18], replicated
- grad_bias: float32 [18], replicated
- grad_up: float32 [18, 512], replicated
All inputs are finite; a program needn't handle non-finite values.
Results may differ from a plain program's by a relative error of at most 0.005.
Values may be sent and summed in bfloat16 or wider, within the bound.
No kernel may reach another device: no remote copies, remote signals or barrier semaphores. Data moves between devices by JAX's collectives and lax.ppermute only.
A program may use at most 128 MiB of HBM per device.

v0:
```python
import jax
import jax.numpy as jnp
from jax import lax
from jax.sharding import PartitionSpec as P

local_weight = 4.0
margin_weight = 4.0


def extended_2(cells, sides, width):
    for axis, dim in sides:
        count = lax.axis_size(axis)
        head = lax.slice_in_dim(cells, 0, width, axis=dim)
        tail = lax.slice_in_dim(cells, cells.shape[dim] - width, cells.shape[dim], axis=dim)
        cells = jnp.concatenate(
            [
                lax.ppermute(tail, axis, [(i, (i + 1) % count) for i in range(count)]),
                cells,
                lax.ppermute(head, axis, [((i + 1) % count, i) for i in range(count)]),
            ],
            axis=dim,
        )
    return cells


def window(extended, rows, cols):
    total = extended[0:rows, 0:cols]
    for first in range(3):
        for second in range(3):
            if first or second:
                total = total + extended[first : first + rows, second : second + cols]
    return total / 9.0


def binary(values):
    return -values * jnp.log(values) - (1.0 - values) * jnp.log1p(-values)


def local(latents, cotangent, w_down, bit_bias, w_up):
    rows, cols, images, width = latents.shape
    bits = w_down.shape[1]
    count = rows * cols * images * lax.axis_size("ha") * lax.axis_size("wa")
    flattened = latents.reshape(-1, width)
    outward = cotangent.reshape(-1, width)
    layers = 1
    logits = jnp.dot(flattened, w_down, preferred_element_type=jnp.float32) + bit_bias
    squash = jax.nn.sigmoid(logits)
    prob = 0.01 + 0.98 * squash
    wide_prob = extended_2(prob.reshape(rows, cols, images, bits), (("ha", 0), ("wa", 1)), layers)
    local_mass = jnp.sum(prob, axis=0) / count
    marginal = lax.psum(local_mass, ("ha", "wa"))
    wide_pooled = window(wide_prob, rows + 2 * layers - 2, cols + 2 * layers - 2)
    slope = local_weight * jnp.log((1.0 - wide_pooled) / wide_pooled)
    wide_slope = extended_2(slope, (("ha", 0), ("wa", 1)), 1)
    bit_entropy = jnp.sum(binary(wide_pooled), axis=-1)
    code = (2.0 * squash - 1.0).astype(jnp.bfloat16)
    code_grad = jnp.dot(outward, w_up.T, preferred_element_type=jnp.float32)
    spread = window(wide_slope, rows, cols).reshape(-1, bits)
    steepness = squash * (1.0 - squash)
    base = ((2.0 * code_grad + 0.98 * spread) * steepness).astype(jnp.bfloat16)
    stacked = jnp.concatenate([base, steepness.astype(jnp.bfloat16)], axis=1)
    latent_part = (
        lax.dot_general(
            flattened, stacked, (((0,), (0,)), ((), ())), preferred_element_type=jnp.float32
        )
        / count
    )
    column_part = jnp.sum(stacked.astype(jnp.float32), axis=0) / count
    up_part = (
        lax.dot_general(code, outward, (((0,), (0,)), ((), ())), preferred_element_type=jnp.float32)
        / count
    )
    latent_total, column_total, grad_up = lax.psum(
        (latent_part, column_part, up_part), ("ha", "wa")
    )
    drift = margin_weight * jnp.log((1.0 - marginal) / marginal)
    logit_grad = ((2.0 * code_grad + 0.98 * (spread - drift)) * steepness).astype(jnp.bfloat16)
    grad_latents = jnp.dot(logit_grad, w_down.T, preferred_element_type=jnp.float32).astype(
        jnp.bfloat16
    )
    grad_latents = grad_latents.reshape(latents.shape)
    grad_down = latent_total[:, :bits] - 0.98 * drift * latent_total[:, bits:]
    grad_bias = column_total[:bits] - 0.98 * drift * column_total[bits:]
    return (grad_latents, bit_entropy, marginal, grad_down, grad_bias, grad_up)


def solution(mesh):
    placed = (P("ha", "wa", None, None), P("ha", "wa", None, None), P(), P(), P())
    return jax.shard_map(
        local,
        mesh=mesh,
        in_specs=placed,
        out_specs=(P("ha", "wa", None, None), P("ha", "wa", None), P(), P(), P(), P()),
        check_vma=False,
    )
```

profile of v0, /device:TPU:8, one launch (start us, length us, event | category | flops | bytes accessed | tf_op | source)
XLA Modules:
  0.0 191.5 jit_solution(5777653072572231376)
XLA Ops:
  7.2 0.7 copy-done
  7.9 5.7 %multiply_add_fusion = (f32[8192,18]{0,1:T(8,128)S(1)}, f32[8192,18]{0,1:T(8,128)S(1)}) fusion(f32[18]{0:T(128)} %param.8, bf16[8192,512]{1,0:T(8,128)(2,1)} %bitcast.26, bf16[512,18]{0,1:T(8,128)(2,1)S(1)} %copy-done), kind=kOutput, calls=%fused_computation.59 | convolution fusion | flops 151879680 | bytes 9586760 | tf_op jit(solution)/shard_map/dot_general | solution.py:46
  13.9 1.8 collective-permute-start.1
  15.6 0.5 reshape.34
  16.1 2.2 %collective-permute-done = f32[1,16,64,18]{2,1,0,3:T(8,128)S(1)} collective-permute-done((f32[1,16,64,18]{2,1,0,3:T(8,128)S(1)}, f32[1,16,64,18]{2,1,0,3:T(8,128)S(1)}, u32[]{:S(2)}, u32[]{:S(2)}) %collective-permute-start) | collective-permute-done | bytes 73760 | tf_op jit(solution)/shard_map/ppermute | solution.py:17
  18.4 0.7 collective-permute-done.1
  19.2 0.1 fusion.42
  19.3 2.0 %collective-permute-start.2 = (f32[10,1,64,18]{2,1,0,3:T(1,128)S(1)}, f32[10,1,64,18]{2,1,0,3:T(1,128)S(1)}, u32[]{:S(2)}, u32[]{:S(2)}) collective-permute-start(f32[10,1,64,18]{2,1,0,3:T(1,128)S(1)} %get-tuple-element.17), channel_id=1, source_target_pairs={{0,1},{1,2},{2,3},{3,0},{4,5},{5,6},{6,7},{7,4},{8,9},{9,10},{10,1... | collective-permute-start | bytes 138248 | tf_op jit(solution)/shard_map/ppermute | solution.py:17
  21.4 1.0 collective-permute-start.3
  22.4 3.3 %collective-permute-done.2 = f32[10,1,64,18]{2,1,0,3:T(1,128)S(1)} collective-permute-done((f32[10,1,64,18]{2,1,0,3:T(1,128)S(1)}, f32[10,1,64,18]{2,1,0,3:T(1,128)S(1)}, u32[]{:S(2)}, u32[]{:S(2)}) %collective-permute-start.2) | collective-permute-done | bytes 46112 | tf_op jit(solution)/shard_map/ppermute | solution.py:17
  25.7 2.5 %collective-permute-done.3 = f32[10,1,64,18]{2,1,0,3:T(1,128)S(1)} collective-permute-done((f32[10,1,64,18]{2,1,0,3:T(1,128)S(1)}, f32[10,1,64,18]{2,1,0,3:T(1,128)S(1)}, u32[]{:S(2)}, u32[]{:S(2)}) %collective-permute-start.3) | collective-permute-done | bytes 46112 | tf_op jit(solution)/shard_map/ppermute | solution.py:19
  28.2 3.1 %fusion.7 = (f32[8,16,64]{2,1,0:T(8,128)}, f32[8,16,64,18]{2,1,0,3:T(8,128)S(1)}) fusion(f32[10,1,64,18]{2,1,0,3:T(1,128)S(1)} %collective-permute-done.3, f32[10,16,64,18]{2,1,0,3:T(8,128)S(1)} %constant_dynamic-update-slice_fusion, f32[1,16,64,18]{2,1,0,3:T(8,128)S(1)} %collective-permute-done.1, f32[8,16,64,18]{2,1,0,3:T(8,128)S(1)} %reshape.34, ...), kind=kLoop, calls=%fused_computation.24 | loop fusion | flops 3383296 | bytes 2189312 | tf_op jit(solution)/shard_map/reduce_sum | solution.py:55
  31.4 0.3 fusion.5
  31.8 1.7 collective-permute-start.5
  33.5 2.8 %collective-permute-done.4 = f32[1,16,64,18]{2,1,0,3:T(8,128)S(1)} collective-permute-done((f32[1,16,64,18]{2,1,0,3:T(8,128)S(1)}, f32[1,16,64,18]{2,1,0,3:T(8,128)S(1)}, u32[]{:S(2)}, u32[]{:S(2)}) %collective-permute-start.4) | collective-permute-done | bytes 73760 | tf_op jit(solution)/shard_map/ppermute | solution.py:17
  36.3 0.7 collective-permute-done.5
  37.0 0.2 pad_maximum_fusion.11
  37.2 1.6 collective-permute-start.6
  38.8 1.4 collective-permute-start.7
  40.2 4.6 %convolution_multiply_fusion.2 = f32[18,512]{1,0:T(8,128)S(1)} fusion(bf16[8192,512]{1,0:T(8,128)(2,1)} %bitcast.24, f32[8192,18]{0,1:T(8,128)S(1)} %get-tuple-element.29), kind=kOutput, calls=%fused_computation.55 | convolution fusion | flops 151446528 | bytes 9015296 | tf_op jit(solution)/shard_map/dot_general | solution.py:70
  44.8 0.4 maximum_maximum_fusion
  45.2 0.7 fusion.21
  45.9 0.4 reshape.35
  46.3 0.3 copy-done.1
  46.7 5.8 %multiply_convert_fusion = (bf16[8192,18]{0,1:T(8,128)(2,1)S(1)}, f32[18]{0:T(128)S(1)}, bf16[8192,18]{0,1:T(8,128)(2,1)S(1)}, f32[8192,18]{0,1:T(8,128)S(1)}) fusion(f32[8192,18]{0,1:T(8,128)S(1)} %reshape.35, f32[8192,18]{0,1:T(8,128)S(1)} %get-tuple-element.29, bf16[8192,512]{1,0:T(8,128)(2,1)} %bitcast.25, bf16[18,512]{1,0:T(8,128)(2,1)S(1)} %copy-done.1), kind=kOutput, calls=%fused_computation.57 | convolution fusion | flops 152616944 | bytes 10766408 | tf_op jit(solution)/shard_map/dot_general | solution.py:57
  52.5 0.3 convert_reduce_fusion
  52.7 5.3 %fusion.25 = f32[512,36]{0,1:T(8,128)} fusion(bf16[8192,512]{1,0:T(8,128)(2,1)} %bitcast.27, bf16[8192,18]{0,1:T(8,128)(2,1)S(1)} %get-tuple-element.23, bf16[8192,18]{0,1:T(8,128)(2,1)S(1)} %get-tuple-element.21), kind=kOutput, calls=%fused_computation.54 | convolution fusion | flops 303187968 | bytes 9052160 | tf_op jit(solution)/shard_map/dot_general | solution.py:63
  58.1 42.2 %all-reduce = (f32[18]{0:T(128)S(1)}, f32[36]{0:T(128)S(1)}, f32[18,512]{1,0:T(8,128)}) all-reduce(f32[18]{0:T(128)S(1)} %broadcast_multiply_fusion.3, f32[36]{0:T(128)S(1)} %broadcast_multiply_fusion, f32[18,512]{1,0:T(8,128)S(1)} %convolution_multiply_fusion.2), channel_id=1, replica_groups=mesh['ha'=8,'wa'=4] {'ha','wa'}, use_global_device_ids=true, to_apply=%region_1.0 | all-reduce | flops 9270 | bytes 74160 | tf_op jit(solution)/shard_map/psum | solution.py:51
  100.2 0.6 multiply_subtract_fusion
  100.8 5.9 %convolution_convert_fusion = bf16[8192,512]{1,0:T(8,128)(2,1)} fusion(bf16[512,18]{0,1:T(8,128)(2,1)S(1)} %copy-done, f32[8192,18]{0,1:T(8,128)S(1)} %get-tuple-element.30, f32[8192,18]{0,1:T(8,128)S(1)} %reshape.35, f32[8192,18]{0,1:T(8,128)S(1)} %get-tuple-element.29, f32[18]{0:T(128)S(1)} %get-tuple-element.27), kind=kOutput, calls=%fused_computation | convolution fusion | flops 156221440 | bytes 10176584 | tf_op jit(solution)/shard_map/dot_general | solution.py:78
  106.7 76.4 %all-reduce.3.cloned.1.call-done = f32[512,36]{0,1:T(8,128)} async-done(((f32[512,36]{0,1:T(8,128)}), f32[512,36]{0,1:T(8,128)}) %all-reduce.3.cloned.1.call-update) | async-done | bytes 73744 | tf_op jit(solution)/shard_map/psum | solution.py:73
  183.1 1.6 fusion.32
  (20 shorter events, 0.5 us)
Async XLA Ops:
  7.2 0.7 copy-start
  7.2 176.0 %all-reduce.3.cloned.1.call-start = ((), (), s32[]{:S(2)}) async-start(), calls=%async_computation | async-start | bytes 163840 | tf_op jit(solution)/shard_map/psum | solution.py:73
  13.7 4.6 %collective-permute-start = (f32[1,16,64,18]{2,1,0,3:T(8,128)S(1)}, f32[1,16,64,18]{2,1,0,3:T(8,128)S(1)}, u32[]{:S(2)}, u32[]{:S(2)}) collective-permute-start(f32[1,16,64,18]{2,1,0,3:T(8,128)S(1)} %bitcast.29), channel_id=1, source_target_pairs={{0,4},{4,8},{8,12},{12,16},{16,20},{20,24},{24,28},{28,0},{1,5},{5... | collective-permute-start | bytes 221192 | tf_op jit(solution)/shard_map/ppermute | solution.py:17
  13.9 5.3 %collective-permute-start.1 = (f32[1,16,64,18]{2,1,0,3:T(8,128)S(1)}, f32[1,16,64,18]{2,1,0,3:T(8,128)S(1)}, u32[]{:S(2)}, u32[]{:S(2)}) collective-permute-start(f32[1,16,64,18]{2,1,0,3:T(8,128)S(1)} %bitcast.30), channel_id=1, source_target_pairs={{4,0},{8,4},{12,8},{16,12},{20,16},{24,20},{28,24},{0,28},{5,1},{9... | collective-permute-start | bytes 221192 | tf_op jit(solution)/shard_map/ppermute | solution.py:19
  19.3 6.4 %collective-permute-start.2 = (f32[10,1,64,18]{2,1,0,3:T(1,128)S(1)}, f32[10,1,64,18]{2,1,0,3:T(1,128)S(1)}, u32[]{:S(2)}, u32[]{:S(2)}) collective-permute-start(f32[10,1,64,18]{2,1,0,3:T(1,128)S(1)} %get-tuple-element.17), channel_id=1, source_target_pairs={{0,1},{1,2},{2,3},{3,0},{4,5},{5,6},{6,7},{7,4},{8,9},{9,10},{10,1... | collective-permute-start | bytes 138248 | tf_op jit(solution)/shard_map/ppermute | solution.py:17
  21.4 6.8 %collective-permute-start.3 = (f32[10,1,64,18]{2,1,0,3:T(1,128)S(1)}, f32[10,1,64,18]{2,1,0,3:T(1,128)S(1)}, u32[]{:S(2)}, u32[]{:S(2)}) collective-permute-start(f32[10,1,64,18]{2,1,0,3:T(1,128)S(1)} %get-tuple-element.18), channel_id=1, source_target_pairs={{1,0},{2,1},{3,2},{0,3},{5,4},{6,5},{7,6},{4,7},{9,8},{10,9},{11,1... | collective-permute-start | bytes 138248 | tf_op jit(solution)/shard_map/ppermute | solution.py:19
  31.7 4.6 %collective-permute-start.4 = (f32[1,16,64,18]{2,1,0,3:T(8,128)S(1)}, f32[1,16,64,18]{2,1,0,3:T(8,128)S(1)}, u32[]{:S(2)}, u32[]{:S(2)}) collective-permute-start(f32[1,16,64,18]{2,1,0,3:T(8,128)S(1)} %get-tuple-element.19), channel_id=1, source_target_pairs={{0,4},{4,8},{8,12},{12,16},{16,20},{20,24},{24,28},{28,0},{1,5},{5... | collective-permute-start | bytes 221192 | tf_op jit(solution)/shard_map/ppermute | solution.py:17
  31.8 5.3 %collective-permute-start.5 = (f32[1,16,64,18]{2,1,0,3:T(8,128)S(1)}, f32[1,16,64,18]{2,1,0,3:T(8,128)S(1)}, u32[]{:S(2)}, u32[]{:S(2)}) collective-permute-start(f32[1,16,64,18]{2,1,0,3:T(8,128)S(1)} %get-tuple-element.20), channel_id=1, source_target_pairs={{4,0},{8,4},{12,8},{16,12},{20,16},{24,20},{28,24},{0,28},{5,1},{9... | collective-permute-start | bytes 221192 | tf_op jit(solution)/shard_map/ppermute | solution.py:19
  37.2 7.6 %collective-permute-start.6 = (f32[10,1,64,18]{2,1,0,3:T(1,128)S(1)}, f32[10,1,64,18]{2,1,0,3:T(1,128)S(1)}, u32[]{:S(2)}, u32[]{:S(2)}) collective-permute-start(f32[10,1,64,18]{2,1,0,3:T(1,128)S(1)} %get-tuple-element.15), channel_id=1, source_target_pairs={{0,1},{1,2},{2,3},{3,0},{4,5},{5,6},{6,7},{7,4},{8,9},{9,10},{10,1... | collective-permute-start | bytes 138248 | tf_op jit(solution)/shard_map/ppermute | solution.py:17
  38.8 6.0 %collective-permute-start.7 = (f32[10,1,64,18]{2,1,0,3:T(1,128)S(1)}, f32[10,1,64,18]{2,1,0,3:T(1,128)S(1)}, u32[]{:S(2)}, u32[]{:S(2)}) collective-permute-start(f32[10,1,64,18]{2,1,0,3:T(1,128)S(1)} %get-tuple-element.16), channel_id=1, source_target_pairs={{1,0},{2,1},{3,2},{0,3},{5,4},{6,5},{7,6},{4,7},{9,8},{10,9},{11,1... | collective-permute-start | bytes 138248 | tf_op jit(solution)/shard_map/ppermute | solution.py:19
  45.9 0.7 copy-start.1
  100.2 6.5 %copy-start.2 = (f32[18]{0:T(128)}, f32[18]{0:T(128)S(1)}, u32[]{:S(2)}) copy-start(f32[18]{0:T(128)S(1)} %get-tuple-element.6) | copy-start | bytes 220
Sparse Core Ops, SparseCore 0:
  58.2 124.8 all-reduce.2
where the time goes:
time: 192 us
  waiting for transfers between devices  88.8 us (46%)
  blocking collectives  42.2 us (22%)
  matrix products  27.2 us (14%)
  between operations  14.2 us (7%)
  starting transfers between devices  9.68 us (5%)
  other arithmetic  7.18 us (4%)
  local copies, waits for them, and re-layouts  2.33 us (1%)
    psum x1, waiting for transfers between devices, local(): lax.psum((latent_part, column_part, up_part), ('ha', 'wa'))  76.4 us
    psum x1, blocking collectives, local(): marginal = lax.psum(local_mass, ('ha', 'wa'))  42.2 us
    ppermute x4, waiting for transfers between devices, extended_2(): lax.ppermute(tail, axis, [(i, (i + 1) % count) for i in range(count)])  8.36 us
    ppermute x4, starting transfers between devices, extended_2(): lax.ppermute(head, axis, [((i + 1) % count, i) for i in range(count)])  5.91 us
    dot_general x1, matrix products, local(): jnp.dot(logit_grad, w_down.T, preferred_element_type=jnp.float32)  5.89 us
    dot_general x1, matrix products, local(): code_grad = jnp.dot(outward, w_up.T, preferred_element_type=jnp.float32)  5.8 us
    dot_general x1, matrix products, local(): jnp.dot(flattened, w_down, preferred_element_type=jnp.float32) + bit_bias  5.7 us
    dot_general x1, matrix products, local(): lax.dot_general(flattened, stacked, (((0,), (0,)), ((), ())), preferred_e...  5.3 us
  transfers between devices with their start and end apart: 9, of which 7 were waited for; matrix products, arithmetic and copies ran while one was open for 6% of the time, Pallas kernels for 0%

commit v1 on v0

--- a/solution.py
+++ b/solution.py
@@ -48,7 +48,8 @@
     prob = 0.01 + 0.98 * squash
     wide_prob = extended_2(prob.reshape(rows, cols, images, bits), (("ha", 0), ("wa", 1)), layers)
     local_mass = jnp.sum(prob, axis=0) / count
-    marginal = lax.psum(local_mass, ("ha", "wa"))
+    inner = lax.psum(local_mass, "wa")
+    marginal = lax.psum(inner, "ha")
     wide_pooled = window(wide_prob, rows + 2 * layers - 2, cols + 2 * layers - 2)
     slope = local_weight * jnp.log((1.0 - wide_pooled) / wide_pooled)
     wide_slope = extended_2(slope, (("ha", 0), ("wa", 1)), 1)

time: 192 us -> 214 us (1.11)
  blocking collectives: 42.2 us -> 64.6 us
    psum x1 -> x3, blocking collectives: 42.2 us -> 64.6 us  [the longest x1 43 us: local(): lax.psum((latent_part, column_part, up_part), ('ha', 'wa'))]
  transfers between devices with their start and end apart: 9 -> 9, of which waited for: 7 -> 7; matrix products, arithmetic and copies ran while one was open for 6% -> 5% of each run, Pallas kernels for 0% -> 0%
where the time goes in v1:
time: 214 us; the launch traced here: 213 us
  waiting for transfers between devices  87.9 us (41%)
  blocking collectives  64.6 us (30%)
  matrix products  27.2 us (13%)
  between operations  14.2 us (7%)
  starting transfers between devices  9.68 us (5%)
  other arithmetic  7.18 us (3%)
  local copies, waits for them, and re-layouts  2.33 us (1%)
    psum x1, waiting for transfers between devices, local(): lax.psum((latent_part, column_part, up_part), ('ha', 'wa'))  75.6 us
    psum x1, blocking collectives, local(): lax.psum((latent_part, column_part, up_part), ('ha', 'wa'))  43 us
    psum x1, blocking collectives, local(): marginal = lax.psum(inner, 'ha')  12.5 us
    psum x1, blocking collectives, local(): inner = lax.psum(local_mass, 'wa')  9.12 us
    ppermute x4, waiting for transfers between devices, extended_2(): lax.ppermute(tail, axis, [(i, (i + 1) % count) for i in range(count)])  8.36 us
    ppermute x4, starting transfers between devices, extended_2(): lax.ppermute(head, axis, [((i + 1) % count, i) for i in range(count)])  5.91 us
    dot_general x1, matrix products, local(): jnp.dot(logit_grad, w_down.T, preferred_element_type=jnp.float32)  5.89 us
    dot_general x1, matrix products, local(): code_grad = jnp.dot(outward, w_up.T, preferred_element_type=jnp.float32)  5.8 us
  transfers between devices with their start and end apart: 9, of which 7 were waited for; matrix products, arithmetic and copies ran while one was open for 5% of the time, Pallas kernels for 0%

profile of v1, /device:TPU:8, one launch (start us, length us, event | category | flops | bytes accessed | tf_op | source)
XLA Modules:
  0.0 213.1 jit_solution(2443750863799765451)
XLA Ops:
  7.2 0.7 copy-done
  7.9 5.7 %multiply_add_fusion = (f32[8192,18]{0,1:T(8,128)S(1)}, f32[8192,18]{0,1:T(8,128)S(1)}) fusion(f32[18]{0:T(128)} %param.8, bf16[8192,512]{1,0:T(8,128)(2,1)} %bitcast.26, bf16[512,18]{0,1:T(8,128)(2,1)S(1)} %copy-done), kind=kOutput, calls=%fused_computation.59 | convolution fusion | flops 151879680 | bytes 9586760 | tf_op jit(solution)/shard_map/dot_general | solution.py:46
  13.9 1.8 collective-permute-start.1
  15.6 0.5 reshape.34
  16.1 2.2 %collective-permute-done = f32[1,16,64,18]{2,1,0,3:T(8,128)S(1)} collective-permute-done((f32[1,16,64,18]{2,1,0,3:T(8,128)S(1)}, f32[1,16,64,18]{2,1,0,3:T(8,128)S(1)}, u32[]{:S(2)}, u32[]{:S(2)}) %collective-permute-start) | collective-permute-done | bytes 73760 | tf_op jit(solution)/shard_map/ppermute | solution.py:17
  18.4 0.7 collective-permute-done.1
  19.3 2.0 collective-permute-start.2
  21.4 1.0 collective-permute-start.3
  22.4 3.3 %collective-permute-done.2 = f32[10,1,64,18]{2,1,0,3:T(1,128)S(1)} collective-permute-done((f32[10,1,64,18]{2,1,0,3:T(1,128)S(1)}, f32[10,1,64,18]{2,1,0,3:T(1,128)S(1)}, u32[]{:S(2)}, u32[]{:S(2)}) %collective-permute-start.2) | collective-permute-done | bytes 46112 | tf_op jit(solution)/shard_map/ppermute | solution.py:17
  25.7 2.5 %collective-permute-done.3 = f32[10,1,64,18]{2,1,0,3:T(1,128)S(1)} collective-permute-done((f32[10,1,64,18]{2,1,0,3:T(1,128)S(1)}, f32[10,1,64,18]{2,1,0,3:T(1,128)S(1)}, u32[]{:S(2)}, u32[]{:S(2)}) %collective-permute-start.3) | collective-permute-done | bytes 46112 | tf_op jit(solution)/shard_map/ppermute | solution.py:19
  28.2 3.1 %fusion.7 = (f32[8,16,64]{2,1,0:T(8,128)}, f32[8,16,64,18]{2,1,0,3:T(8,128)S(1)}) fusion(f32[10,1,64,18]{2,1,0,3:T(1,128)S(1)} %collective-permute-done.3, f32[10,16,64,18]{2,1,0,3:T(8,128)S(1)} %constant_dynamic-update-slice_fusion, f32[1,16,64,18]{2,1,0,3:T(8,128)S(1)} %collective-permute-done.1, f32[8,16,64,18]{2,1,0,3:T(8,128)S(1)} %reshape.34, ...), kind=kLoop, calls=%fused_computation.24 | loop fusion | flops 3383296 | bytes 2189312 | tf_op jit(solution)/shard_map/reduce_sum | solution.py:56
  31.4 0.3 fusion.5
  31.8 1.7 collective-permute-start.5
  33.5 2.8 %collective-permute-done.4 = f32[1,16,64,18]{2,1,0,3:T(8,128)S(1)} collective-permute-done((f32[1,16,64,18]{2,1,0,3:T(8,128)S(1)}, f32[1,16,64,18]{2,1,0,3:T(8,128)S(1)}, u32[]{:S(2)}, u32[]{:S(2)}) %collective-permute-start.4) | collective-permute-done | bytes 73760 | tf_op jit(solution)/shard_map/ppermute | solution.py:17
  36.3 0.7 collective-permute-done.5
  37.2 1.6 collective-permute-start.6
  38.8 1.4 collective-permute-start.7
  40.2 4.6 %convolution_multiply_fusion.2 = f32[18,512]{1,0:T(8,128)S(1)} fusion(bf16[8192,512]{1,0:T(8,128)(2,1)} %bitcast.24, f32[8192,18]{0,1:T(8,128)S(1)} %get-tuple-element.28), kind=kOutput, calls=%fused_computation.55 | convolution fusion | flops 151446528 | bytes 9015296 | tf_op jit(solution)/shard_map/dot_general | solution.py:71
  44.8 0.4 maximum_maximum_fusion
  45.2 0.7 fusion.21
  45.9 0.4 reshape.35
  46.3 0.3 copy-done.1
  46.7 5.8 %fusion.39 = (f32[18]{0:T(128)S(1)}, bf16[8192,18]{0,1:T(8,128)(2,1)S(1)}, bf16[8192,18]{0,1:T(8,128)(2,1)S(1)}, f32[8192,18]{0,1:T(8,128)S(1)}) fusion(f32[8192,18]{0,1:T(8,128)S(1)} %get-tuple-element.28, f32[8192,18]{0,1:T(8,128)S(1)} %reshape.35, bf16[8192,512]{1,0:T(8,128)(2,1)} %bitcast.25, bf16[18,512]{1,0:T(8,128)(2,1)S(1)} %copy-done.1), kind=kOutput, calls=%fused_computation.87 | convolution fusion | flops 152616944 | bytes 10766408 | tf_op jit(solution)/shard_map/dot_general | solution.py:58
  52.5 5.3 %fusion.25 = f32[512,36]{0,1:T(8,128)} fusion(bf16[8192,512]{1,0:T(8,128)(2,1)} %bitcast.27, bf16[8192,18]{0,1:T(8,128)(2,1)S(1)} %get-tuple-element.22, bf16[8192,18]{0,1:T(8,128)(2,1)S(1)} %get-tuple-element.21), kind=kOutput, calls=%fused_computation.54 | convolution fusion | flops 303187968 | bytes 9052160 | tf_op jit(solution)/shard_map/dot_general | solution.py:64
  57.7 0.3 convert_reduce_fusion
  58.0 9.1 %psum.35 = f32[18]{0:T(128)S(1)} all-reduce(f32[18]{0:T(128)S(1)} %broadcast_multiply_fusion.3), channel_id=1, replica_groups=mesh['ha'=8,'wa'=4] {'wa'}, use_global_device_ids=true, to_apply=%region_1.0 | all-reduce | flops 18 | bytes 144 | tf_op jit(solution)/shard_map/psum | solution.py:51
  67.1 12.5 %psum.36 = f32[18]{0:T(128)S(1)} all-reduce(f32[18]{0:T(128)S(1)} %psum.35), channel_id=1, replica_groups=mesh['ha'=8,'wa'=4] {'ha'}, use_global_device_ids=true, to_apply=%region_2.0 | all-reduce | flops 18 | bytes 144 | tf_op jit(solution)/shard_map/psum | solution.py:52
  79.7 43.0 %all-reduce = (f32[36]{0:T(128)S(1)}, f32[18,512]{1,0:T(8,128)}) all-reduce(f32[36]{0:T(128)S(1)} %broadcast_multiply_fusion, f32[18,512]{1,0:T(8,128)S(1)} %convolution_multiply_fusion.2), channel_id=1, replica_groups=mesh['ha'=8,'wa'=4] {'ha','wa'}, use_global_device_ids=true, to_apply=%region_6.0 | all-reduce | flops 9252 | bytes 74016 | tf_op jit(solution)/shard_map/psum | solution.py:74
  122.7 0.6 multiply_subtract_fusion
  123.2 5.9 %convolution_convert_fusion = bf16[8192,512]{1,0:T(8,128)(2,1)} fusion(bf16[512,18]{0,1:T(8,128)(2,1)S(1)} %copy-done, f32[8192,18]{0,1:T(8,128)S(1)} %get-tuple-element.29, f32[8192,18]{0,1:T(8,128)S(1)} %reshape.35, f32[8192,18]{0,1:T(8,128)S(1)} %get-tuple-element.28, f32[18]{0:T(128)S(1)} %get-tuple-element.26), kind=kOutput, calls=%fused_computation | convolution fusion | flops 156221440 | bytes 10176584 | tf_op jit(solution)/shard_map/dot_general | solution.py:79
  129.1 75.6 %all-reduce.3.cloned.1.call-done = f32[512,36]{0,1:T(8,128)} async-done(((f32[512,36]{0,1:T(8,128)}), f32[512,36]{0,1:T(8,128)}) %all-reduce.3.cloned.1.call-update) | async-done | bytes 73744 | tf_op jit(solution)/shard_map/psum | solution.py:74
  204.7 1.6 fusion.32
  (22 shorter events, 0.8 us)
Async XLA Ops:
  7.2 0.7 copy-start
  7.2 197.5 %all-reduce.3.cloned.1.call-start = ((), (), s32[]{:S(2)}) async-start(), calls=%async_computation | async-start | bytes 163840 | tf_op jit(solution)/shard_map/psum | solution.py:74
  13.7 4.6 %collective-permute-start = (f32[1,16,64,18]{2,1,0,3:T(8,128)S(1)}, f32[1,16,64,18]{2,1,0,3:T(8,128)S(1)}, u32[]{:S(2)}, u32[]{:S(2)}) collective-permute-start(f32[1,16,64,18]{2,1,0,3:T(8,128)S(1)} %bitcast.29), channel_id=1, source_target_pairs={{0,4},{4,8},{8,12},{12,16},{16,20},{20,24},{24,28},{28,0},{1,5},{5... | collective-permute-start | bytes 221192 | tf_op jit(solution)/shard_map/ppermute | solution.py:17
  13.9 5.3 %collective-permute-start.1 = (f32[1,16,64,18]{2,1,0,3:T(8,128)S(1)}, f32[1,16,64,18]{2,1,0,3:T(8,128)S(1)}, u32[]{:S(2)}, u32[]{:S(2)}) collective-permute-start(f32[1,16,64,18]{2,1,0,3:T(8,128)S(1)} %bitcast.30), channel_id=1, source_target_pairs={{4,0},{8,4},{12,8},{16,12},{20,16},{24,20},{28,24},{0,28},{5,1},{9... | collective-permute-start | bytes 221192 | tf_op jit(solution)/shard_map/ppermute | solution.py:19
  19.3 6.4 %collective-permute-start.2 = (f32[10,1,64,18]{2,1,0,3:T(1,128)S(1)}, f32[10,1,64,18]{2,1,0,3:T(1,128)S(1)}, u32[]{:S(2)}, u32[]{:S(2)}) collective-permute-start(f32[10,1,64,18]{2,1,0,3:T(1,128)S(1)} %get-tuple-element.16), channel_id=1, source_target_pairs={{0,1},{1,2},{2,3},{3,0},{4,5},{5,6},{6,7},{7,4},{8,9},{9,10},{10,1... | collective-permute-start | bytes 138248 | tf_op jit(solution)/shard_map/ppermute | solution.py:17
  21.4 6.8 %collective-permute-start.3 = (f32[10,1,64,18]{2,1,0,3:T(1,128)S(1)}, f32[10,1,64,18]{2,1,0,3:T(1,128)S(1)}, u32[]{:S(2)}, u32[]{:S(2)}) collective-permute-start(f32[10,1,64,18]{2,1,0,3:T(1,128)S(1)} %get-tuple-element.17), channel_id=1, source_target_pairs={{1,0},{2,1},{3,2},{0,3},{5,4},{6,5},{7,6},{4,7},{9,8},{10,9},{11,1... | collective-permute-start | bytes 138248 | tf_op jit(solution)/shard_map/ppermute | solution.py:19
  31.7 4.6 %collective-permute-start.4 = (f32[1,16,64,18]{2,1,0,3:T(8,128)S(1)}, f32[1,16,64,18]{2,1,0,3:T(8,128)S(1)}, u32[]{:S(2)}, u32[]{:S(2)}) collective-permute-start(f32[1,16,64,18]{2,1,0,3:T(8,128)S(1)} %get-tuple-element.18), channel_id=1, source_target_pairs={{0,4},{4,8},{8,12},{12,16},{16,20},{20,24},{24,28},{28,0},{1,5},{5... | collective-permute-start | bytes 221192 | tf_op jit(solution)/shard_map/ppermute | solution.py:17
  31.8 5.3 %collective-permute-start.5 = (f32[1,16,64,18]{2,1,0,3:T(8,128)S(1)}, f32[1,16,64,18]{2,1,0,3:T(8,128)S(1)}, u32[]{:S(2)}, u32[]{:S(2)}) collective-permute-start(f32[1,16,64,18]{2,1,0,3:T(8,128)S(1)} %get-tuple-element.19), channel_id=1, source_target_pairs={{4,0},{8,4},{12,8},{16,12},{20,16},{24,20},{28,24},{0,28},{5,1},{9... | collective-permute-start | bytes 221192 | tf_op jit(solution)/shard_map/ppermute | solution.py:19
  37.2 7.6 %collective-permute-start.6 = (f32[10,1,64,18]{2,1,0,3:T(1,128)S(1)}, f32[10,1,64,18]{2,1,0,3:T(1,128)S(1)}, u32[]{:S(2)}, u32[]{:S(2)}) collective-permute-start(f32[10,1,64,18]{2,1,0,3:T(1,128)S(1)} %get-tuple-element.14), channel_id=1, source_target_pairs={{0,1},{1,2},{2,3},{3,0},{4,5},{5,6},{6,7},{7,4},{8,9},{9,10},{10,1... | collective-permute-start | bytes 138248 | tf_op jit(solution)/shard_map/ppermute | solution.py:17
  38.8 6.0 %collective-permute-start.7 = (f32[10,1,64,18]{2,1,0,3:T(1,128)S(1)}, f32[10,1,64,18]{2,1,0,3:T(1,128)S(1)}, u32[]{:S(2)}, u32[]{:S(2)}) collective-permute-start(f32[10,1,64,18]{2,1,0,3:T(1,128)S(1)} %get-tuple-element.15), channel_id=1, source_target_pairs={{1,0},{2,1},{3,2},{0,3},{5,4},{6,5},{7,6},{4,7},{9,8},{10,9},{11,1... | collective-permute-start | bytes 138248 | tf_op jit(solution)/shard_map/ppermute | solution.py:19
  45.9 0.7 copy-start.1
  79.6 49.5 %copy-start.2 = (f32[18]{0:T(128)}, f32[18]{0:T(128)S(1)}, u32[]{:S(2)}) copy-start(f32[18]{0:T(128)S(1)} %psum.36) | copy-start | bytes 220
Sparse Core Ops, SparseCore 0:
  79.8 124.8 all-reduce.2
